TPU v7x, 128 devices: a whole 4x4x4 slice. The times are simulated.
128 devices in a mesh: lat: 16 (over x, z_lo, core), lon: 8 (over z_hi, y).
Axes of the slice: x: 4, y: 4, z: 4 (z_hi: 2, z_lo: 2; z = z_hi * 2 + z_lo), core: 2. Of those that a mesh axis runs over, the one named last changes fastest.
Arguments:
- x_tiles: bfloat16 [8, 64, 77, 256], P('lon', 'lat'), may hold values from -6 to 6
- tile_pos: int32 [8, 64], P('lon', 'lat'), may hold values from 0 to 511, as said below
- valid_rows: int32 [8, 64], P('lon', 'lat'), may hold values from 1 to 16
- stem_w: bfloat16 [77, 200], replicated, may hold values from -0.625 to 0.625
- dw_kernel: float32 [200, 49], replicated, may hold values from -0.875 to 0.875
- norm_gain: float32 [200], replicated, may hold values from 0.1 to 1.9
- w_in: bfloat16 [200, 800], replicated, may hold values from -0.4375 to 0.4375
- w_out: bfloat16 [800, 200], replicated, may hold values from -0.21875 to 0.21875
- cotangent: bfloat16 [8, 64, 200, 256], P('lon', 'lat'), may hold values from -3072 to 3072
Outputs:
- out_tiles: bfloat16 [8, 64, 200, 256], P('lon', 'lat')
- grad_w_in: float32 [200, 800], replicated
- grad_w_out: float32 [800, 200], replicated
- grad_kernel: float32 [200, 49], replicated
- grad_gain: float32 [200], replicated
Inputs may be any that keep to these rules, and one draw needn't show every extreme that they name: `tile_pos`: in each sector the places are distinct; in the order of place, the r-th active tile of a sector is held by lat index r % 16. At most 2 tiles of one device lie in one band block of 32 tiles, and this is reached; some band block is fully active in every sector.
All inputs are finite; a program needn't handle non-finite values.
Results may differ from a plain program's by a relative error of at most 0.0075.
Values may be sent and summed in bfloat16 or wider, within the bound.
No kernel may reach another device: no remote copies, remote signals or barrier semaphores. Data moves between devices by JAX's collectives and lax.ppermute only.
A program may use at most 128 MiB of HBM per device.

v0:
```python
import jax
import jax.numpy as jnp
from jax import lax
from jax.sharding import PartitionSpec as P

C = 200
CIN = 77
KW = 7
TS = 16
BH = 64
BW = 128
K_TILES = 32


def extended(block, sides, width, periodic):
    for axis, dim in sides:
        count = lax.axis_size(axis)
        forward = [(i, i + 1) for i in range(count - 1)]
        if periodic:
            forward.append((count - 1, 0))
        backward = [(target, source) for source, target in forward]
        low = lax.ppermute(
            lax.slice_in_dim(block, block.shape[dim] - width, None, axis=dim), axis, forward
        )
        high = lax.ppermute(lax.slice_in_dim(block, 0, width, axis=dim), axis, backward)
        block = jnp.concatenate([low, block, high], axis=dim)
    return block


def gelu_tanh(value):
    return jax.nn.gelu(value, approximate=True)


def tiles_to_block(tiles):
    chan = tiles.shape[1]
    shaped = tiles.reshape(BH // TS, BW // TS, chan, TS, TS)
    return shaped.transpose(2, 0, 3, 1, 4).reshape(chan, BH, BW)


def block_to_tiles(block):
    chan = block.shape[0]
    shaped = block.reshape(chan, BH // TS, TS, BW // TS, TS)
    return shaped.transpose(1, 3, 0, 2, 4).reshape(K_TILES, chan, TS * TS)


def select_rows(onehot, tiles):
    return jnp.einsum("qa,acp->qcp", onehot, tiles, preferred_element_type=jnp.float32).astype(
        jnp.bfloat16
    )


def body(x_tiles, tile_pos, valid_rows, stem_w, dw_kernel, norm_gain, w_in, w_out, cotangent):
    f32 = jnp.float32
    bf16 = jnp.bfloat16
    lat_count = lax.axis_size("lat")
    per_pair = (K_TILES + lat_count - 1) // lat_count
    slot_count = lat_count * per_pair
    cells = TS * TS
    inputs = x_tiles[0]
    places = tile_pos[0]
    ocean_rows = valid_rows[0]
    upstream = cotangent[0]
    tile_count = inputs.shape[0]
    cell_rows = jnp.arange(cells, dtype=jnp.int32) // TS
    ocean = cell_rows[None, :] < ocean_rows[:, None]
    masked_in = jnp.where(ocean[:, None, :], inputs, jnp.zeros_like(inputs))
    stem_tiles = jnp.einsum("kc,akp->acp", stem_w, masked_in, preferred_element_type=f32).astype(
        bf16
    )
    band_of = places // K_TILES
    local_place = places - band_of * K_TILES
    tile_order = jnp.arange(tile_count, dtype=jnp.int32)
    earlier = (band_of[None, :] == band_of[:, None]) & (tile_order[None, :] < tile_order[:, None])
    rank_in = jnp.sum(earlier.astype(jnp.int32), axis=1)
    slot_of = band_of * per_pair + rank_in
    route_map = jnp.arange(slot_count, dtype=jnp.int32)[:, None] == slot_of[None, :]
    route_b = route_map.astype(bf16)
    slot_place = jnp.sum(jnp.where(route_map, local_place[None, :] + 1, 0), axis=1) - 1
    slot_place = slot_place.reshape(lat_count, per_pair)
    outgoing = select_rows(route_b, masked_in).reshape(lat_count, per_pair, CIN, cells)
    arrived_raw, arrived_place = (
        lax.all_to_all(outgoing, "lat", split_axis=0, concat_axis=0, tiled=True),
        lax.all_to_all(slot_place, "lat", split_axis=0, concat_axis=0, tiled=True),
    )
    arrived_raw = arrived_raw.reshape(slot_count, CIN, cells)
    arrived = jnp.einsum("kc,akp->acp", stem_w, arrived_raw, preferred_element_type=f32).astype(
        bf16
    )
    placing = (
        jnp.arange(K_TILES, dtype=jnp.int32)[:, None] == arrived_place.reshape(slot_count)[None, :]
    )
    placing_b = placing.astype(bf16)
    band_field = tiles_to_block(select_rows(placing_b, arrived))
    reach = KW // 2
    widened = extended(band_field, (("lon", 2),), reach, True)
    padded = extended(widened, (("lat", 1),), reach, False)

    def window(tap_index):
        row_off = tap_index // KW
        col_off = tap_index % KW
        return padded[:, row_off : row_off + BH, col_off : col_off + BW].astype(f32)

    conv_out = jnp.zeros(band_field.shape, f32)
    for tap_index in range(KW * KW):
        conv_out = conv_out + dw_kernel[:, tap_index][:, None, None] * window(tap_index)
    centred = conv_out - jnp.mean(conv_out, axis=0, keepdims=True)
    inv_std = lax.rsqrt(jnp.mean(centred * centred, axis=0, keepdims=True) + 1e-06)
    unit = centred * inv_std
    normed = (unit * norm_gain[:, None, None]).astype(bf16)
    returning = select_rows(placing_b.T, block_to_tiles(normed)).reshape(
        lat_count, per_pair, C, cells
    )
    returned = lax.all_to_all(returning, "lat", split_axis=0, concat_axis=0, tiled=True).reshape(
        slot_count, C, cells
    )
    features = select_rows(route_b.T, returned)
    preact = jnp.einsum("ch,acp->ahp", w_in, features, preferred_element_type=f32)
    hidden = gelu_tanh(preact).astype(bf16)
    branch = jnp.einsum("hc,ahp->acp", w_out, hidden, preferred_element_type=f32)
    result = jnp.where(ocean[:, None, :], stem_tiles.astype(f32) + branch, 0.0).astype(bf16)
    masked_grad = jnp.where(ocean[:, None, :], upstream, jnp.zeros_like(upstream))
    grad_hidden = jnp.einsum("hc,acp->ahp", w_out, masked_grad, preferred_element_type=f32)
    grad_preact = jax.vjp(gelu_tanh, preact)[1](grad_hidden)[0].astype(bf16)
    grad_feats = jnp.einsum("ch,ahp->acp", w_in, grad_preact, preferred_element_type=f32).astype(
        bf16
    )
    grad_outgoing = select_rows(route_b, grad_feats).reshape(lat_count, per_pair, C, cells)
    grad_arrived = lax.all_to_all(
        grad_outgoing, "lat", split_axis=0, concat_axis=0, tiled=True
    ).reshape(slot_count, C, cells)
    sum_in = jnp.einsum("acp,ahp->ch", features, grad_preact, preferred_element_type=f32)
    sum_out = jnp.einsum("ahp,acp->hc", hidden, masked_grad, preferred_element_type=f32)
    grad_field = tiles_to_block(select_rows(placing_b, grad_arrived)).astype(f32)
    scaled = grad_field * norm_gain[:, None, None]
    grad_conv = inv_std * (
        scaled
        - jnp.mean(scaled, axis=0, keepdims=True)
        - unit * jnp.mean(scaled * unit, axis=0, keepdims=True)
    )
    kernel_terms = []
    for tap_index in range(KW * KW):
        kernel_terms.append(jnp.sum(grad_conv * window(tap_index), axis=(1, 2)))
    sum_kernel = jnp.stack(kernel_terms, axis=1)
    sum_gain = jnp.sum(grad_field * unit, axis=(1, 2))
    cell_sum = TS * jnp.sum(ocean_rows.astype(f32))
    total_in, total_out, total_kernel, total_gain, cell_total = lax.psum(
        (sum_in, sum_out, sum_kernel, sum_gain, cell_sum), ("lat", "lon")
    )
    return (
        result[None],
        total_in / cell_total,
        total_out / cell_total,
        total_kernel / cell_total,
        total_gain / cell_total,
    )


def solution(mesh):
    in_specs = (
        P("lon", "lat", None, None),
        P("lon", "lat"),
        P("lon", "lat"),
        P(),
        P(),
        P(),
        P(),
        P(),
        P("lon", "lat", None, None),
    )
    out_specs = (P("lon", "lat", None, None), P(), P(), P(), P())
    return jax.shard_map(body, mesh=mesh, in_specs=in_specs, out_specs=out_specs, check_vma=False)
```

profile of v0, /device:TPU:2, one launch (start us, length us, event | category | flops | bytes accessed | tf_op | source)
XLA Modules:
  0.0 583.2 jit_solution(11858804636175604378)
XLA Ops:
  9.6 6.2 %all-to-all-start = ((s32[16,1,2]{2,1,0:T(1,128)}), s32[16,1,2]{2,1,0:T(1,128)S(1)}, u32[]{:S(2)}, u32[]{:S(2)}) async-start(s32[16,1,2]{2,1,0:T(1,128)} %bitcast.9), calls=%async_computation | async-start | bytes 16384 | tf_op jit(solution)/shard_map/all_to_all | solution.py:83
  20.5 5.7 all-to-all-start.1
  27.6 15.3 %all-to-all-done.1 = bf16[16,2,77,256]{3,1,2,0:T(2,128)(2,1)S(1)} async-done(((bf16[16,2,77,256]{3,1,2,0:T(2,128)(2,1)}), bf16[16,2,77,256]{3,1,2,0:T(2,128)(2,1)S(1)}, u32[]{:S(2)}, u32[]{:S(2)}) %all-to-all-start.1) | async-done | bytes 1261600 | tf_op jit(solution)/shard_map/all_to_all | solution.py:82
  46.9 7.2 %copy.72 = bf16[32,200,256]{1,2,0:T(8,128)(2,1)} copy(bf16[32,200,256]{2,0,1:T(8,128)(2,1)} %fusion.114) | data formatting | bytes 6553600 | tf_op jit(solution)/shard_map/convert_element_type | solution.py:47
  58.7 4.5 collective-permute-start.1
  68.4 4.7 collective-permute-start.3
  76.2 8.1 %maximum_maximum_fusion = (bf16[200,67,134]{0,2,1:T(8,128)(2,1)S(1)}, bf16[200,67,134]{0,2,1:T(8,128)(2,1)S(1)}) fusion(bf16[200,64,3]{0,2,1:T(4,128)(2,1)S(1)} %collective-permute-done.1, bf16[200,64,128]{0,2,1:T(8,128)(2,1)S(1)} %bitcast.228, bf16[200,64,3]{0,2,1:T(4,128)(2,1)S(1)} %collective-permute-done, ...), kind=kLoop, calls=%fused_computation.208 | loop fusion | flops 28729600 | bytes 10934400 | tf_op jit(solution)/shard_map/concatenate | solution.py:26
  84.3 68.1 %fusion.152 = (f32[64,128]{1,0:T(8,128)S(1)}, f32[200,64,128]{0,2,1:T(8,128)S(1)}) fusion(bf16[200,67,134]{0,2,1:T(8,128)(2,1)S(1)} %get-tuple-element.77, f32[200]{0:T(256)S(1)} %bitcast.286, f32[200]{0:T(256)S(1)} %bitcast.287, f32[200]{0:T(256)S(1)} %bitcast.240, f32[200]{0:T(256)S(1)} %bitcast.241, f32[200]{0:T(256)S(1)} %bitcast.242, ...), kind=kLoop, calls=%fused_computation.307 | loop fusion | flops 270327808 | bytes 147681568 | tf_op jit(solution)/shard_map/reduce_sum | solution.py:106
  160.2 7.3 %copy.76 = bf16[32,200,256]{2,0,1:T(8,128)(2,1)} copy(bf16[32,200,256]{1,2,0:T(8,128)(2,1)} %bitcast.237) | data formatting | bytes 6553600 | tf_op jit(solution)/shard_map/reshape | solution.py:43
  167.4 4.8 convolution_convert_fusion.1
  172.2 7.5 %reshape.217 = bf16[16,2,200,256]{3,1,0,2:T(2,128)(2,1)} reshape(bf16[32,200,256]{2,0,1:T(8,128)(2,1)} %convolution_convert_fusion.1) | data formatting | bytes 6553600 | tf_op jit(solution)/shard_map/reshape | solution.py:110
  179.8 4.2 copy.77
  183.9 45.5 %all_to_all.21 = bf16[16,2,200,256]{3,1,2,0:T(2,128)(2,1)S(1)} all-to-all(bf16[16,2,200,256]{3,1,2,0:T(2,128)(2,1)S(1)} %copy.77), channel_id=1, replica_groups=mesh['lat'=16,'lon'=8] {'lat'}, dimensions={0} | all-to-all | bytes 6553600 | tf_op jit(solution)/shard_map/all_to_all | solution.py:113
  229.4 5.5 copy.78
  234.9 7.8 %reshape.218 = bf16[32,200,256]{2,0,1:T(8,128)(2,1)} reshape(bf16[16,2,200,256]{3,1,0,2:T(2,128)(2,1)} %copy.78) | data formatting | bytes 6553600 | tf_op jit(solution)/shard_map/reshape | solution.py:113
  253.1 7.6 %reshape.219 = bf16[16,2,200,256]{3,1,0,2:T(2,128)(2,1)} reshape(bf16[32,200,256]{2,0,1:T(8,128)(2,1)} %convolution_convert_fusion) | data formatting | bytes 6553600 | tf_op jit(solution)/shard_map/reshape | solution.py:127
  260.7 5.8 %copy.82 = bf16[16,2,200,256]{3,1,2,0:T(2,128)(2,1)} copy(bf16[16,2,200,256]{3,1,0,2:T(2,128)(2,1)} %reshape.219) | data formatting | bytes 6553600 | tf_op jit(solution)/shard_map/reshape | solution.py:127
  266.5 6.0 %all-to-all-start.3 = ((bf16[16,2,200,256]{3,1,2,0:T(2,128)(2,1)}), bf16[16,2,200,256]{3,1,2,0:T(2,128)(2,1)}, u32[]{:S(2)}, u32[]{:S(2)}) async-start(bf16[16,2,200,256]{3,1,2,0:T(2,128)(2,1)} %copy.82), calls=%async_computation.3 | async-start | bytes 6553600 | tf_op jit(solution)/shard_map/all_to_all | solution.py:128
  276.7 4.2 convolution_bitcast_fusion
  285.0 27.7 %all-to-all-done.3 = bf16[16,2,200,256]{3,1,2,0:T(2,128)(2,1)} async-done(((bf16[16,2,200,256]{3,1,2,0:T(2,128)(2,1)}), bf16[16,2,200,256]{3,1,2,0:T(2,128)(2,1)}, u32[]{:S(2)}, u32[]{:S(2)}) %all-to-all-start.3) | async-done | bytes 3276832 | tf_op jit(solution)/shard_map/all_to_all | solution.py:128
  312.7 7.5 %copy.83 = bf16[16,2,200,256]{3,1,0,2:T(2,128)(2,1)} copy(bf16[16,2,200,256]{3,1,2,0:T(2,128)(2,1)} %all-to-all-done.3) | data formatting | bytes 6553600 | tf_op jit(solution)/shard_map/all_to_all | solution.py:128
  320.1 7.8 %reshape.220 = bf16[32,200,256]{2,0,1:T(8,128)(2,1)} reshape(bf16[16,2,200,256]{3,1,0,2:T(2,128)(2,1)} %copy.83) | data formatting | bytes 6553600 | tf_op jit(solution)/shard_map/reshape | solution.py:130
  327.9 5.7 convert_convert_fusion
  333.6 9.3 %copy.84 = f32[32,200,256]{1,2,0:T(8,128)} copy(f32[32,200,256]{2,0,1:T(8,128)} %convert_convert_fusion) | data formatting | bytes 13107200 | tf_op jit(solution)/shard_map/convert_element_type | solution.py:133
  342.9 4.6 multiply_reduce_fusion.2
  347.7 4.4 copy.85
  352.1 8.8 %multiply_reduce_fusion = (f32[200]{0:T(256)S(1)}, f32[64,128]{1,0:T(8,128)S(1)}) fusion(f32[200,64,128]{0,2,1:T(8,128)S(1)} %bitcast.231, f32[200,64,128]{0,2,1:T(8,128)} %copy-done.4, f32[64,128]{1,0:T(8,128)S(1)} %add_rsqrt_fusion, f32[64,128]{1,0:T(8,128)S(1)} %broadcast_multiply_fusion.1, f32[200]{0:T(256)S(1)} %copy-done.12), kind=kLoop, calls=%fused_computation.195 | loop fusion | flops 11460408 | bytes 13207104 | tf_op jit(solution)/shard_map/reduce_sum | solution.py:144
  360.9 50.6 %fusion.96 = (f32[200]{0:T(256)S(1)}, f32[200]{0:T(256)S(1)}, f32[200]{0:T(256)S(1)}, f32[200]{0:T(256)S(1)}, f32[200]{0:T(256)S(1)}, /*index=5*/f32[200]{0:T(25...) fusion(bf16[200,67,134]{0,2,1:T(8,128)(2,1)} %copy-done.3, ...), kind=kLoop, calls=%fused_computation.194 | loop fusion | flops 99938800 | bytes 78789472 | tf_op jit(solution)/shard_map/reduce_sum | solution.py:142
  411.5 49.7 %fusion.45 = (f32[200]{0:T(256)S(1)}, f32[200]{0:T(256)S(1)}, f32[200]{0:T(256)S(1)}, f32[200]{0:T(256)S(1)}, f32[200]{0:T(256)S(1)}, /*index=5*/f32[200]{0:T(25...) fusion(f32[200,64,128]{0,2,1:T(8,128)} %get-tuple-element.71, ...), kind=kLoop, calls=%fused_computation.143 | loop fusion | flops 88470000 | bytes 65550400 | tf_op jit(solution)/shard_map/reduce_sum | solution.py:142
  461.3 27.5 %fusion.78 = (f32[200]{0:T(256)S(1)}, f32[200]{0:T(256)S(1)}, f32[200]{0:T(256)S(1)}, f32[200]{0:T(256)S(1)}, f32[200]{0:T(256)S(1)}, /*index=5*/f32[200]{0:T(25...) fusion(f32[200,64,128]{0,2,1:T(8,128)} %get-tuple-element.71, ...), kind=kLoop, calls=%fused_computation.176 | loop fusion | flops 78641200 | bytes 19822400 | tf_op jit(solution)/shard_map/reduce_sum | solution.py:142
  488.9 4.3 fusion.27
  493.4 74.8 %all-reduce = (f32[]{:T(128)}, f32[200,49]{0,1:T(8,128)S(1)}, f32[200]{0:T(256)S(1)}) all-reduce(f32[]{:T(128)S(6)} %mul_shard_map.3, f32[200,49]{0,1:T(8,128)S(1)} %stack.199, f32[200]{0:T(256)S(1)} %get-tuple-element.5), channel_id=1, replica_groups=mesh['lat'=16,'lon'=8] {'lat','lon'}, use_global_device_ids=true, to_apply=%region_6.7 | all-reduce | flops 10001 | bytes 80008 | tf_op jit(solution)/shard_map/psum | solution.py:146
  (93 shorter events, 59.1 us)
Async XLA Ops:
  7.2 238.1 %copy-start = (bf16[200,800]{1,0:T(8,128)(2,1)S(1)}, bf16[200,800]{1,0:T(8,128)(2,1)}, u32[]{:S(2)}) copy-start(bf16[200,800]{1,0:T(8,128)(2,1)} %param.15) | copy-start | bytes 960004
  7.2 19.1 %copy-start.11 = (f32[200,49]{0,1:T(8,128)S(1)}, f32[200,49]{0,1:T(8,128)}, u32[]{:S(2)}) copy-start(f32[200,49]{0,1:T(8,128)} %param.13) | copy-start | bytes 117604
  7.2 35.9 %copy-start.10 = (bf16[77,200]{1,0:T(8,128)(2,1)S(1)}, bf16[77,200]{1,0:T(8,128)(2,1)}, u32[]{:S(2)}) copy-start(bf16[77,200]{1,0:T(8,128)(2,1)} %param.12) | copy-start | bytes 92404
  9.6 11.0 %all-to-all-start = ((s32[16,1,2]{2,1,0:T(1,128)}), s32[16,1,2]{2,1,0:T(1,128)S(1)}, u32[]{:S(2)}, u32[]{:S(2)}) async-start(s32[16,1,2]{2,1,0:T(1,128)} %bitcast.9), calls=%async_computation | async-start | bytes 16384 | tf_op jit(solution)/shard_map/all_to_all | solution.py:83
  20.5 22.4 %all-to-all-start.1 = ((bf16[16,2,77,256]{3,1,2,0:T(2,128)(2,1)}), bf16[16,2,77,256]{3,1,2,0:T(2,128)(2,1)S(1)}, u32[]{:S(2)}, u32[]{:S(2)}) async-start(bf16[16,2,77,256]{3,1,2,0:T(2,128)(2,1)} %copy.69), calls=%async_computation.1 | async-start | bytes 2523136 | tf_op jit(solution)/shard_map/all_to_all | solution.py:82
  56.9 27.4 %copy-start.6 = (bf16[200,4,16,8,16]{0,4,3,2,1:T(8,128)(2,1)}, bf16[200,4,16,8,16]{0,4,3,2,1:T(8,128)(2,1)S(1)}, u32[]{:S(2)}) copy-start(bf16[200,4,16,8,16]{0,4,3,2,1:T(8,128)(2,1)S(1)} %copy.73) | copy-start | bytes 9830404
  57.0 9.3 %collective-permute-start = (bf16[200,64,3]{0,2,1:T(4,128)(2,1)S(1)}, bf16[200,64,3]{0,2,1:T(4,128)(2,1)S(1)}, u32[]{:S(2)}, u32[]{:S(2)}) collective-permute-start(bf16[200,64,3]{0,2,1:T(4,128)(2,1)S(1)} %get-tuple-element.80), channel_id=1, source_target_pairs={{0,1},{1,2},{2,3},{3,4},{4,5},{5,6},{6,7},{7,0},{8,9},{9,10},{10,1... | collective-permute-start | bytes 230408 | tf_op jit(solution)/shard_map/ppermute | solution.py:22
  58.7 7.6 %collective-permute-start.1 = (bf16[200,64,3]{0,2,1:T(4,128)(2,1)S(1)}, bf16[200,64,3]{0,2,1:T(4,128)(2,1)S(1)}, u32[]{:S(2)}, u32[]{:S(2)}) collective-permute-start(bf16[200,64,3]{0,2,1:T(4,128)(2,1)S(1)} %get-tuple-element.81), channel_id=1, source_target_pairs={{1,0},{2,1},{3,2},{4,3},{5,4},{6,5},{7,6},{0,7},{9,8},{10,9},{11,1... | collective-permute-start | bytes 230408 | tf_op jit(solution)/shard_map/ppermute | solution.py:25
  66.5 8.0 %collective-permute-start.2 = (bf16[200,3,134]{0,2,1:T(8,128)(2,1)S(1)}, bf16[200,3,134]{0,2,1:T(8,128)(2,1)S(1)}, u32[]{:S(2)}, u32[]{:S(2)}) collective-permute-start(bf16[200,3,134]{0,2,1:T(8,128)(2,1)S(1)} %get-tuple-element.78), channel_id=1, source_target_pairs={{0,8},{8,16},{16,24},{24,32},{32,40},{40,48},{48,56},{56,64},{64,7... | collective-permute-start | bytes 482408 | tf_op jit(solution)/shard_map/ppermute | solution.py:22
  68.4 7.8 %collective-permute-start.3 = (bf16[200,3,134]{0,2,1:T(8,128)(2,1)S(1)}, bf16[200,3,134]{0,2,1:T(8,128)(2,1)S(1)}, u32[]{:S(2)}, u32[]{:S(2)}) collective-permute-start(bf16[200,3,134]{0,2,1:T(8,128)(2,1)S(1)} %get-tuple-element.79), channel_id=1, source_target_pairs={{8,0},{16,8},{24,16},{32,24},{40,32},{48,40},{56,48},{64,56},{72,6... | collective-permute-start | bytes 482408 | tf_op jit(solution)/shard_map/ppermute | solution.py:25
  84.3 68.1 %copy-start.2 = (bf16[200,67,134]{0,2,1:T(8,128)(2,1)}, bf16[200,67,134]{0,2,1:T(8,128)(2,1)S(1)}, u32[]{:S(2)}) copy-start(bf16[200,67,134]{0,2,1:T(8,128)(2,1)S(1)} %get-tuple-element.76) | copy-start | bytes 10773604
  84.3 68.1 %copy-start.3 = (bf16[200,67,134]{0,2,1:T(8,128)(2,1)}, bf16[200,67,134]{0,2,1:T(8,128)(2,1)S(1)}, u32[]{:S(2)}) copy-start(bf16[200,67,134]{0,2,1:T(8,128)(2,1)S(1)} %get-tuple-element.77) | copy-start | bytes 10773604
  152.5 5.1 copy-start.4
  152.5 2.5 copy-start.12
  234.9 11.0 %copy-start.14 = (bf16[800,200]{0,1:T(8,128)(2,1)S(1)}, bf16[800,200]{0,1:T(8,128)(2,1)}, u32[]{:S(2)}) copy-start(bf16[800,200]{0,1:T(8,128)(2,1)} %param.16) | copy-start | bytes 960004
  246.0 3.7 copy-start.8
  253.1 19.4 %copy-start.13 = (s32[1,4]{1,0:T(1,128)S(1)}, s32[1,4]{1,0:T(1,128)}, u32[]{:S(2)}) copy-start(s32[1,4]{1,0:T(1,128)} %param.11) | copy-start | bytes 52
  266.5 46.1 %all-to-all-start.3 = ((bf16[16,2,200,256]{3,1,2,0:T(2,128)(2,1)}), bf16[16,2,200,256]{3,1,2,0:T(2,128)(2,1)}, u32[]{:S(2)}, u32[]{:S(2)}) async-start(bf16[16,2,200,256]{3,1,2,0:T(2,128)(2,1)} %copy.82), calls=%async_computation.3 | async-start | bytes 6553600 | tf_op jit(solution)/shard_map/all_to_all | solution.py:128
  272.5 295.6 %all-reduce.4.cloned.1.call-start = ((), (), s32[]{:S(2)}) async-start(), calls=%async_computation.4 | async-start | bytes 2867200 | tf_op jit(solution)/shard_map/psum | solution.py:146
  276.7 4.3 copy-start.9
  352.1 8.8 %copy-start.7 = (f32[200,4,16,8,16]{0,4,3,2,1:T(8,128)}, f32[200,4,16,8,16]{0,4,3,2,1:T(8,128)S(1)}, u32[]{:S(2)}) copy-start(f32[200,4,16,8,16]{0,4,3,2,1:T(8,128)S(1)} %copy.85) | copy-start | bytes 19660804
  360.9 127.9 %slice-start = ((s8[4665344]{0:T(1024)(128)(4,1)}), s8[471040]{0:T(1024)(128)(4,1)S(1)}, s32[]{:S(2)}) async-start(s8[4665344]{0:T(1024)(128)(4,1)} %bitcast.224), calls=%async_computation.5 | async-start | bytes 942080
  411.5 77.3 %slice-start.1 = ((s8[4665344]{0:T(1024)(128)(4,1)}), s8[4194304]{0:T(1024)(128)(4,1)S(1)}, s32[]{:S(2)}) async-start(s8[4665344]{0:T(1024)(128)(4,1)} %bitcast.224), calls=%async_computation.6 | async-start | bytes 8388608
  461.3 27.6 %copy-start.5 = (f32[200,64,128]{0,2,1:T(8,128)S(1)}, f32[200,64,128]{0,2,1:T(8,128)}, u32[]{:S(2)}) copy-start(f32[200,64,128]{0,2,1:T(8,128)} %get-tuple-element.71) | copy-start | bytes 19660804
  461.3 114.9 %copy-start.1 = (bf16[200,800]{1,0:T(8,128)(2,1)S(1)}, bf16[200,800]{1,0:T(8,128)(2,1)}, u32[]{:S(2)}) copy-start(bf16[200,800]{1,0:T(8,128)(2,1)} %param.15) | copy-start | bytes 960004
Sparse Core Ops, SparseCore 0:
  281.1 168.1 all-reduce.3
where the time goes:
time: 590 us; the launch traced here: 583 us
  other arithmetic  240 us (41%)
  blocking collectives  120 us (20%)
  local copies, waits for them, and re-layouts  91.8 us (16%)
  waiting for transfers between devices  49.2 us (8%)
  matrix products  36.2 us (6%)
  starting transfers between devices  30.8 us (5%)
  between operations  15.4 us (3%)
    reduce_sum x4, other arithmetic, body(): kernel_terms.append(jnp.sum(grad_conv * window(tap_index), axis=(1, 2)))  132 us
    psum x1, blocking collectives, body(): lax.psum((sum_in, sum_out, sum_kernel, sum_gain, cell_sum), ('lat', 'lon'))  74.8 us
    reduce_sum x1, other arithmetic, body(): centred = conv_out - jnp.mean(conv_out, axis=0, keepdims=True)  68.1 us
    all_to_all x1, blocking collectives, body(): lax.all_to_all(returning, 'lat', split_axis=0, concat_axis=0, tiled=True)  45.5 us
    all_to_all x1, waiting for transfers between devices, body(): lax.all_to_all(grad_outgoing, 'lat', split_axis=0, concat_axis=0, tiled=T...  27.7 us
    dot_general x6, matrix products, select_rows(): jnp.einsum('qa,acp->qcp', onehot, tiles, preferred_element_type=jnp.float32)  19.1 us
    all_to_all x1, waiting for transfers between devices, body(): lax.all_to_all(outgoing, 'lat', split_axis=0, concat_axis=0, tiled=True)  15.3 us
    convert_element_type x2, local copies, waits for them, and re-layouts, body(): tiles_to_block(select_rows(placing_b, grad_arrived)).astype(f32)  13.7 us
  transfers between devices with their start and end apart: 8, of which 5 were waited for; matrix products, arithmetic and copies ran while one was open for 34% of the time, Pallas kernels for 0%

commit v1 on v0

--- a/solution.py
+++ b/solution.py
@@ -144,7 +144,7 @@
     sum_gain = jnp.sum(grad_field * unit, axis=(1, 2))
     cell_sum = TS * jnp.sum(ocean_rows.astype(f32))
     total_in, total_out, total_kernel, total_gain, cell_total = lax.psum(
-        (sum_in, sum_out, sum_kernel, sum_gain, cell_sum), ("lat", "lon")
+        lax.psum((sum_in, sum_out, sum_kernel, sum_gain, cell_sum), "lat"), "lon"
     )
     return (
         result[None],

time: 590 us -> 721 us (1.22)
  waiting for transfers between devices: 49.2 us -> 151 us
  blocking collectives: 120 us -> 143 us
    psum x1 -> x2, waiting for transfers between devices: 0.01 us -> 130 us  [the longest x1 130 us: body(): lax.psum((sum_in, sum_out, sum_kernel, sum_gain, cell_sum), 'lat')]
    all_to_all x1, waiting for transfers between devices: 27.7 us -> 0.01 us  [body(): lax.all_to_all(grad_outgoing, 'lat', split_axis=0, concat_axis=0, tiled=T...]
    psum x1 -> x2, blocking collectives: 74.8 us -> 97.9 us  [the longest x1 55.7 us: body(): lax.psum((sum_in, sum_out, sum_kernel, sum_gain, cell_sum), 'lat')]
  transfers between devices with their start and end apart: 8 -> 9, of which waited for: 5 -> 5; matrix products, arithmetic and copies ran while one was open for 34% -> 28% of each run, Pallas kernels for 0% -> 0%
where the time goes in v1:
time: 721 us; the launch traced here: 707 us
  other arithmetic  240 us (33%)
  waiting for transfers between devices  151 us (21%)
  blocking collectives  143 us (20%)
  local copies, waits for them, and re-layouts  91.8 us (13%)
  matrix products  35.2 us (5%)
  starting transfers between devices  30.8 us (4%)
  between operations  15.4 us (2%)
    reduce_sum x4, other arithmetic, body(): kernel_terms.append(jnp.sum(grad_conv * window(tap_index), axis=(1, 2)))  132 us
    psum x1, waiting for transfers between devices, body(): lax.psum((sum_in, sum_out, sum_kernel, sum_gain, cell_sum), 'lat')  130 us
    reduce_sum x1, other arithmetic, body(): centred = conv_out - jnp.mean(conv_out, axis=0, keepdims=True)  68.1 us
    psum x1, blocking collectives, body(): lax.psum((sum_in, sum_out, sum_kernel, sum_gain, cell_sum), 'lat')  55.7 us
    all_to_all x1, blocking collectives, body(): lax.all_to_all(returning, 'lat', split_axis=0, concat_axis=0, tiled=True)  45.5 us
    psum x1, blocking collectives, body(): lax.psum(lax.psum((sum_in, sum_out, sum_kernel, sum_gain, cell_sum), 'lat...  42.2 us
    dot_general x6, matrix products, select_rows(): jnp.einsum('qa,acp->qcp', onehot, tiles, preferred_element_type=jnp.float32)  19.1 us
    all_to_all x1, waiting for transfers between devices, body(): lax.all_to_all(outgoing, 'lat', split_axis=0, concat_axis=0, tiled=True)  15.3 us
  transfers between devices with their start and end apart: 9, of which 5 were waited for; matrix products, arithmetic and copies ran while one was open for 28% of the time, Pallas kernels for 0%

profile of v1, /device:TPU:2, one launch (start us, length us, event | category | flops | bytes accessed | tf_op | source)
XLA Modules:
  0.0 707.4 jit_solution(13745555626973874189)
XLA Ops:
  9.6 6.2 all-to-all-start
  20.5 5.7 all-to-all-start.1
  27.6 15.3 %all-to-all-done.1 = bf16[16,2,77,256]{3,1,2,0:T(2,128)(2,1)S(1)} async-done(((bf16[16,2,77,256]{3,1,2,0:T(2,128)(2,1)}), bf16[16,2,77,256]{3,1,2,0:T(2,128)(2,1)S(1)}, u32[]{:S(2)}, u32[]{:S(2)}) %all-to-all-start.1) | async-done | bytes 1261600 | tf_op jit(solution)/shard_map/all_to_all | solution.py:82
  46.9 7.2 %copy.72 = bf16[32,200,256]{1,2,0:T(8,128)(2,1)} copy(bf16[32,200,256]{2,0,1:T(8,128)(2,1)} %fusion.114) | data formatting | bytes 6553600 | tf_op jit(solution)/shard_map/convert_element_type | solution.py:47
  58.7 4.5 collective-permute-start.1
  68.4 4.7 collective-permute-start.3
  76.2 8.1 %maximum_maximum_fusion = (bf16[200,67,134]{0,2,1:T(8,128)(2,1)S(1)}, bf16[200,67,134]{0,2,1:T(8,128)(2,1)S(1)}) fusion(bf16[200,64,3]{0,2,1:T(4,128)(2,1)S(1)} %collective-permute-done.1, bf16[200,64,128]{0,2,1:T(8,128)(2,1)S(1)} %bitcast.228, bf16[200,64,3]{0,2,1:T(4,128)(2,1)S(1)} %collective-permute-done, ...), kind=kLoop, calls=%fused_computation.208 | loop fusion | flops 28729600 | bytes 10934400 | tf_op jit(solution)/shard_map/concatenate | solution.py:26
  84.3 68.1 %fusion.152 = (f32[64,128]{1,0:T(8,128)S(1)}, f32[200,64,128]{0,2,1:T(8,128)S(1)}) fusion(bf16[200,67,134]{0,2,1:T(8,128)(2,1)S(1)} %get-tuple-element.82, f32[200]{0:T(256)S(1)} %bitcast.286, f32[200]{0:T(256)S(1)} %bitcast.287, f32[200]{0:T(256)S(1)} %bitcast.240, f32[200]{0:T(256)S(1)} %bitcast.241, f32[200]{0:T(256)S(1)} %bitcast.242, ...), kind=kLoop, calls=%fused_computation.307 | loop fusion | flops 270327808 | bytes 147681568 | tf_op jit(solution)/shard_map/reduce_sum | solution.py:106
  160.2 7.3 %copy.76 = bf16[32,200,256]{2,0,1:T(8,128)(2,1)} copy(bf16[32,200,256]{1,2,0:T(8,128)(2,1)} %bitcast.237) | data formatting | bytes 6553600 | tf_op jit(solution)/shard_map/reshape | solution.py:43
  167.4 4.8 convolution_convert_fusion.1
  172.2 7.5 %reshape.217 = bf16[16,2,200,256]{3,1,0,2:T(2,128)(2,1)} reshape(bf16[32,200,256]{2,0,1:T(8,128)(2,1)} %convolution_convert_fusion.1) | data formatting | bytes 6553600 | tf_op jit(solution)/shard_map/reshape | solution.py:110
  179.8 4.2 copy.77
  183.9 45.5 %all_to_all.21 = bf16[16,2,200,256]{3,1,2,0:T(2,128)(2,1)S(1)} all-to-all(bf16[16,2,200,256]{3,1,2,0:T(2,128)(2,1)S(1)} %copy.77), channel_id=1, replica_groups=mesh['lat'=16,'lon'=8] {'lat'}, dimensions={0} | all-to-all | bytes 6553600 | tf_op jit(solution)/shard_map/all_to_all | solution.py:113
  229.4 5.5 copy.78
  234.9 7.8 %reshape.218 = bf16[32,200,256]{2,0,1:T(8,128)(2,1)} reshape(bf16[16,2,200,256]{3,1,0,2:T(2,128)(2,1)} %copy.78) | data formatting | bytes 6553600 | tf_op jit(solution)/shard_map/reshape | solution.py:113
  253.1 7.5 %reshape.219 = bf16[16,2,200,256]{3,1,0,2:T(2,128)(2,1)} reshape(bf16[32,200,256]{2,0,1:T(8,128)(2,1)} %convolution_convert_fusion) | data formatting | bytes 6553600 | tf_op jit(solution)/shard_map/reshape | solution.py:127
  260.7 5.8 copy.82
  266.5 6.0 all-to-all-start.3
  284.0 129.6 %all-reduce.7.cloned.1.call-done = (f32[200,800]{1,0:T(8,128)}, f32[800,200]{0,1:T(8,128)}) async-done(((f32[200,800]{1,0:T(8,128)}, f32[800,200]{0,1:T(8,128)}), (f32[200,800]{1,0:T(8,128)}, f32[800,200]{0,1:T(8,128)})) %all-reduce.7.cloned.1.call-update) | async-done | bytes 1280016 | tf_op jit(solution)/shard_map/psum | solution.py:147
  413.7 7.4 %copy.83 = bf16[16,2,200,256]{3,1,0,2:T(2,128)(2,1)} copy(bf16[16,2,200,256]{3,1,2,0:T(2,128)(2,1)} %all-to-all-done.3) | data formatting | bytes 6553600 | tf_op jit(solution)/shard_map/all_to_all | solution.py:128
  421.1 7.8 %reshape.220 = bf16[32,200,256]{2,0,1:T(8,128)(2,1)} reshape(bf16[16,2,200,256]{3,1,0,2:T(2,128)(2,1)} %copy.83) | data formatting | bytes 6553600 | tf_op jit(solution)/shard_map/reshape | solution.py:130
  428.9 5.6 convert_convert_fusion
  434.5 9.3 %copy.84 = f32[32,200,256]{1,2,0:T(8,128)} copy(f32[32,200,256]{2,0,1:T(8,128)} %convert_convert_fusion) | data formatting | bytes 13107200 | tf_op jit(solution)/shard_map/convert_element_type | solution.py:133
  443.8 4.6 multiply_reduce_fusion.2
  448.7 4.5 copy.85
  453.1 8.8 %multiply_reduce_fusion = (f32[200]{0:T(256)S(1)}, f32[64,128]{1,0:T(8,128)S(1)}) fusion(f32[200,64,128]{0,2,1:T(8,128)S(1)} %bitcast.231, f32[200,64,128]{0,2,1:T(8,128)} %copy-done.4, f32[64,128]{1,0:T(8,128)S(1)} %add_rsqrt_fusion, f32[64,128]{1,0:T(8,128)S(1)} %broadcast_multiply_fusion.1, f32[200]{0:T(256)S(1)} %copy-done.11), kind=kLoop, calls=%fused_computation.195 | loop fusion | flops 11460408 | bytes 13207104 | tf_op jit(solution)/shard_map/reduce_sum | solution.py:144
  462.0 50.6 %fusion.96 = (f32[200]{0:T(256)S(1)}, f32[200]{0:T(256)S(1)}, f32[200]{0:T(256)S(1)}, f32[200]{0:T(256)S(1)}, f32[200]{0:T(256)S(1)}, /*index=5*/f32[200]{0:T(25...) fusion(bf16[200,67,134]{0,2,1:T(8,128)(2,1)} %copy-done.3, ...), kind=kLoop, calls=%fused_computation.194 | loop fusion | flops 99938800 | bytes 78789472 | tf_op jit(solution)/shard_map/reduce_sum | solution.py:142
  512.6 49.7 %fusion.45 = (f32[200]{0:T(256)S(1)}, f32[200]{0:T(256)S(1)}, f32[200]{0:T(256)S(1)}, f32[200]{0:T(256)S(1)}, f32[200]{0:T(256)S(1)}, /*index=5*/f32[200]{0:T(25...) fusion(f32[200,64,128]{0,2,1:T(8,128)} %get-tuple-element.76, ...), kind=kLoop, calls=%fused_computation.143 | loop fusion | flops 88470000 | bytes 65550400 | tf_op jit(solution)/shard_map/reduce_sum | solution.py:142
  562.3 27.5 %fusion.78 = (f32[200]{0:T(256)S(1)}, f32[200]{0:T(256)S(1)}, f32[200]{0:T(256)S(1)}, f32[200]{0:T(256)S(1)}, f32[200]{0:T(256)S(1)}, /*index=5*/f32[200]{0:T(25...) fusion(f32[200,64,128]{0,2,1:T(8,128)} %get-tuple-element.76, ...), kind=kLoop, calls=%fused_computation.176 | loop fusion | flops 78641200 | bytes 19822400 | tf_op jit(solution)/shard_map/reduce_sum | solution.py:142
  589.9 4.3 fusion.27
  594.4 55.7 %all-reduce = (f32[]{:T(128)}, f32[200,49]{0,1:T(8,128)S(1)}, f32[200]{0:T(256)S(1)}) all-reduce(f32[]{:T(128)S(6)} %mul_shard_map.3, f32[200,49]{0,1:T(8,128)S(1)} %stack.199, f32[200]{0:T(256)S(1)} %get-tuple-element.5), channel_id=1, replica_groups=mesh['lat'=16,'lon'=8] {'lat'}, use_global_device_ids=true, to_apply=%region_7.8 | all-reduce | flops 10001 | bytes 80008 | tf_op jit(solution)/shard_map/psum | solution.py:147
  650.1 42.2 %all-reduce.2 = (f32[]{:T(128)}, f32[200,49]{0,1:T(8,128)S(1)}, f32[200]{0:T(256)S(1)}) all-reduce(f32[]{:T(128)} %get-tuple-element.66, f32[200,49]{0,1:T(8,128)S(1)} %get-tuple-element.67, f32[200]{0:T(256)S(1)} %get-tuple-element.68), channel_id=1, replica_groups=mesh['lat'=16,'lon'=8] {'lon'}, use_global_device_ids=true, to_apply=%region_8.9 | all-reduce | flops 10001 | bytes 80008 | tf_op jit(solution)/shard_map/psum | solution.py:146
  (95 shorter events, 62.4 us)
Async XLA Ops:
  7.2 238.1 %copy-start = (bf16[200,800]{1,0:T(8,128)(2,1)S(1)}, bf16[200,800]{1,0:T(8,128)(2,1)}, u32[]{:S(2)}) copy-start(bf16[200,800]{1,0:T(8,128)(2,1)} %param.15) | copy-start | bytes 960004
  7.2 19.1 %copy-start.10 = (f32[200,49]{0,1:T(8,128)S(1)}, f32[200,49]{0,1:T(8,128)}, u32[]{:S(2)}) copy-start(f32[200,49]{0,1:T(8,128)} %param.13) | copy-start | bytes 117604
  7.2 35.9 %copy-start.9 = (bf16[77,200]{1,0:T(8,128)(2,1)S(1)}, bf16[77,200]{1,0:T(8,128)(2,1)}, u32[]{:S(2)}) copy-start(bf16[77,200]{1,0:T(8,128)(2,1)} %param.12) | copy-start | bytes 92404
  9.6 11.0 %all-to-all-start = ((s32[16,1,2]{2,1,0:T(1,128)}), s32[16,1,2]{2,1,0:T(1,128)S(1)}, u32[]{:S(2)}, u32[]{:S(2)}) async-start(s32[16,1,2]{2,1,0:T(1,128)} %bitcast.9), calls=%async_computation | async-start | bytes 16384 | tf_op jit(solution)/shard_map/all_to_all | solution.py:83
  20.5 22.4 %all-to-all-start.1 = ((bf16[16,2,77,256]{3,1,2,0:T(2,128)(2,1)}), bf16[16,2,77,256]{3,1,2,0:T(2,128)(2,1)S(1)}, u32[]{:S(2)}, u32[]{:S(2)}) async-start(bf16[16,2,77,256]{3,1,2,0:T(2,128)(2,1)} %copy.69), calls=%async_computation.1 | async-start | bytes 2523136 | tf_op jit(solution)/shard_map/all_to_all | solution.py:82
  56.9 27.4 %copy-start.6 = (bf16[200,4,16,8,16]{0,4,3,2,1:T(8,128)(2,1)}, bf16[200,4,16,8,16]{0,4,3,2,1:T(8,128)(2,1)S(1)}, u32[]{:S(2)}) copy-start(bf16[200,4,16,8,16]{0,4,3,2,1:T(8,128)(2,1)S(1)} %copy.73) | copy-start | bytes 9830404
  57.0 9.3 %collective-permute-start = (bf16[200,64,3]{0,2,1:T(4,128)(2,1)S(1)}, bf16[200,64,3]{0,2,1:T(4,128)(2,1)S(1)}, u32[]{:S(2)}, u32[]{:S(2)}) collective-permute-start(bf16[200,64,3]{0,2,1:T(4,128)(2,1)S(1)} %get-tuple-element.85), channel_id=1, source_target_pairs={{0,1},{1,2},{2,3},{3,4},{4,5},{5,6},{6,7},{7,0},{8,9},{9,10},{10,1... | collective-permute-start | bytes 230408 | tf_op jit(solution)/shard_map/ppermute | solution.py:22
  58.7 7.6 %collective-permute-start.1 = (bf16[200,64,3]{0,2,1:T(4,128)(2,1)S(1)}, bf16[200,64,3]{0,2,1:T(4,128)(2,1)S(1)}, u32[]{:S(2)}, u32[]{:S(2)}) collective-permute-start(bf16[200,64,3]{0,2,1:T(4,128)(2,1)S(1)} %get-tuple-element.86), channel_id=1, source_target_pairs={{1,0},{2,1},{3,2},{4,3},{5,4},{6,5},{7,6},{0,7},{9,8},{10,9},{11,1... | collective-permute-start | bytes 230408 | tf_op jit(solution)/shard_map/ppermute | solution.py:25
  66.5 8.0 %collective-permute-start.2 = (bf16[200,3,134]{0,2,1:T(8,128)(2,1)S(1)}, bf16[200,3,134]{0,2,1:T(8,128)(2,1)S(1)}, u32[]{:S(2)}, u32[]{:S(2)}) collective-permute-start(bf16[200,3,134]{0,2,1:T(8,128)(2,1)S(1)} %get-tuple-element.83), channel_id=1, source_target_pairs={{0,8},{8,16},{16,24},{24,32},{32,40},{40,48},{48,56},{56,64},{64,7... | collective-permute-start | bytes 482408 | tf_op jit(solution)/shard_map/ppermute | solution.py:22
  68.4 7.8 %collective-permute-start.3 = (bf16[200,3,134]{0,2,1:T(8,128)(2,1)S(1)}, bf16[200,3,134]{0,2,1:T(8,128)(2,1)S(1)}, u32[]{:S(2)}, u32[]{:S(2)}) collective-permute-start(bf16[200,3,134]{0,2,1:T(8,128)(2,1)S(1)} %get-tuple-element.84), channel_id=1, source_target_pairs={{8,0},{16,8},{24,16},{32,24},{40,32},{48,40},{56,48},{64,56},{72,6... | collective-permute-start | bytes 482408 | tf_op jit(solution)/shard_map/ppermute | solution.py:25
  84.3 68.1 %copy-start.2 = (bf16[200,67,134]{0,2,1:T(8,128)(2,1)}, bf16[200,67,134]{0,2,1:T(8,128)(2,1)S(1)}, u32[]{:S(2)}) copy-start(bf16[200,67,134]{0,2,1:T(8,128)(2,1)S(1)} %get-tuple-element.81) | copy-start | bytes 10773604
  84.3 68.1 %copy-start.3 = (bf16[200,67,134]{0,2,1:T(8,128)(2,1)}, bf16[200,67,134]{0,2,1:T(8,128)(2,1)S(1)}, u32[]{:S(2)}) copy-start(bf16[200,67,134]{0,2,1:T(8,128)(2,1)S(1)} %get-tuple-element.82) | copy-start | bytes 10773604
  152.5 5.1 copy-start.4
  152.5 2.5 copy-start.11
  234.9 11.0 %copy-start.13 = (bf16[800,200]{0,1:T(8,128)(2,1)S(1)}, bf16[800,200]{0,1:T(8,128)(2,1)}, u32[]{:S(2)}) copy-start(bf16[800,200]{0,1:T(8,128)(2,1)} %param.16) | copy-start | bytes 960004
  246.0 3.7 copy-start.8
  266.5 147.1 %all-to-all-start.3 = ((bf16[16,2,200,256]{3,1,2,0:T(2,128)(2,1)}), bf16[16,2,200,256]{3,1,2,0:T(2,128)(2,1)}, u32[]{:S(2)}, u32[]{:S(2)}) async-start(bf16[16,2,200,256]{3,1,2,0:T(2,128)(2,1)} %copy.82), calls=%async_computation.3 | async-start | bytes 6553600 | tf_op jit(solution)/shard_map/all_to_all | solution.py:128
  272.5 5.9 copy-start.12
  272.5 141.1 %all-reduce.7.cloned.1.call-start = ((), (), s32[]{:S(2)}) async-start(), calls=%async_computation.4 | async-start | bytes 2867200 | tf_op jit(solution)/shard_map/psum | solution.py:147
  278.4 413.9 %all-reduce.9.cloned.1.call-start = ((), (), s32[]{:S(2)}) async-start(), calls=%async_computation.5 | async-start | bytes 2867200 | tf_op jit(solution)/shard_map/psum | solution.py:146
  453.1 8.8 %copy-start.7 = (f32[200,4,16,8,16]{0,4,3,2,1:T(8,128)}, f32[200,4,16,8,16]{0,4,3,2,1:T(8,128)S(1)}, u32[]{:S(2)}) copy-start(f32[200,4,16,8,16]{0,4,3,2,1:T(8,128)S(1)} %copy.85) | copy-start | bytes 19660804
  461.9 127.9 %slice-start = ((s8[4665344]{0:T(1024)(128)(4,1)}), s8[471040]{0:T(1024)(128)(4,1)S(1)}, s32[]{:S(2)}) async-start(s8[4665344]{0:T(1024)(128)(4,1)} %bitcast.224), calls=%async_computation.6 | async-start | bytes 942080
  512.5 77.3 %slice-start.1 = ((s8[4665344]{0:T(1024)(128)(4,1)}), s8[4194304]{0:T(1024)(128)(4,1)S(1)}, s32[]{:S(2)}) async-start(s8[4665344]{0:T(1024)(128)(4,1)} %bitcast.224), calls=%async_computation.7 | async-start | bytes 8388608
  562.3 27.6 %copy-start.5 = (f32[200,64,128]{0,2,1:T(8,128)S(1)}, f32[200,64,128]{0,2,1:T(8,128)}, u32[]{:S(2)}) copy-start(f32[200,64,128]{0,2,1:T(8,128)} %get-tuple-element.76) | copy-start | bytes 19660804
  562.3 138.0 %copy-start.1 = (bf16[200,800]{1,0:T(8,128)(2,1)S(1)}, bf16[200,800]{1,0:T(8,128)(2,1)}, u32[]{:S(2)}) copy-start(bf16[200,800]{1,0:T(8,128)(2,1)} %param.15) | copy-start | bytes 960004
Sparse Core Ops, SparseCore 0:
  278.5 135.0 all-reduce.6
  416.2 96.4 all-reduce.8
